TPU v7x, 32 devices: a whole 2x2x4 slice. The times are simulated.
32 devices in a mesh: seq: 16 (over z, y, core), head: 2 (over x).
Axes of the slice: x: 2, y: 2, z: 4, core: 2. Of those that a mesh axis runs over, the one named last changes fastest.
Arguments:
- qkv: bfloat16 [3, 2048, 1024], P(None, ('seq', 'head')), may hold values from -128 to 128
- token_rate: float32 [2048, 2], P('seq', 'head'), may hold values from 0.1 to 1
- head_rate: float32 [2], P('head'), may hold values from 0.5 to 2
- fast_state: float32 [3, 2, 512, 512], P(None, 'head', 'seq'), may hold values from -0.25 to 0.25
Outputs:
- combined: bfloat16 [2048, 1024], P(('seq', 'head'))
- new_state: float32 [3, 2, 512, 512], P(None, 'head', 'seq')
All inputs are finite; a program needn't handle non-finite values.
Results may differ from a plain program's by a relative error of at most 0.017.
Values may be sent and summed in bfloat16 or wider, within the bound.
A program may use at most 64 MiB of HBM per device.

v0:
```python
import jax
import jax.numpy as jnp
from jax import lax
from jax.sharding import PartitionSpec as P

WINDOW = 1024
NS_STEPS = 2
ns_first = 3.4445
ns_second = -4.775
ns_third = 2.0315
rms_eps = 1e-06
norm_eps = 1e-07
precise = lax.Precision.HIGHEST


def from_behind(block, axis, distance):
    devices = range(lax.axis_size(axis))
    route = [(i - distance, i) for i in devices if i - distance in devices]
    return lax.ppermute(block, axis, route)


def rms_scaled(values):
    return values * lax.rsqrt(jnp.mean(values * values, axis=-1, keepdims=True) + rms_eps)


def contract_last(left_side, right_side):
    return lax.dot_general(
        left_side, right_side, (((1,), (1,)), ((), ())), preferred_element_type=jnp.float32
    )


def contract_first(left_side, right_side):
    return lax.dot_general(
        left_side, right_side, (((0,), (0,)), ((), ())), preferred_element_type=jnp.float32
    )


def head_gradient(key_norm, signal, weight_piece):
    gate_act = contract_last(key_norm, weight_piece[0])
    up_act = contract_last(key_norm, weight_piece[1])
    active = (jax.nn.silu(gate_act) * up_act).astype(jnp.bfloat16)
    back_grad = contract_last(signal, weight_piece[2])
    sigmoid_gate = jax.nn.sigmoid(gate_act)
    grad_gate = (
        back_grad * up_act * sigmoid_gate * (1.0 + gate_act * (1.0 - sigmoid_gate))
    ).astype(jnp.bfloat16)
    grad_up = (back_grad * jax.nn.silu(gate_act)).astype(jnp.bfloat16)
    return jnp.stack(
        [
            contract_first(grad_gate, key_norm),
            contract_first(grad_up, key_norm),
            contract_first(active, signal),
        ]
    )


def gram_times(gram_matrix, section_number, row_block):
    if section_number == 0:
        return jnp.einsum("mij,mjk->mik", row_block, gram_matrix, precision=precise)
    once_moved = gram_times(gram_matrix, section_number - 1, row_block)
    return poly_times(
        gram_matrix, section_number - 1, poly_times(gram_matrix, section_number - 1, once_moved)
    )


def poly_times(gram_matrix, section_number, row_block):
    moved_once = gram_times(gram_matrix, section_number, row_block)
    moved_twice = gram_times(gram_matrix, section_number, moved_once)
    return ns_first * row_block + ns_second * moved_once + ns_third * moved_twice


def shards(qkv, token_rate, head_rate, fast_state):
    grouped = lax.all_to_all(qkv, "head", split_axis=2, concat_axis=1, tiled=True)
    tok_rows = grouped.shape[1]
    head_dim = grouped.shape[2]
    seq_index = lax.axis_index("seq")
    state_rows = fast_state.shape[2]
    query_norm = rms_scaled(grouped[0].astype(jnp.float32)).astype(jnp.bfloat16)
    key_norm = rms_scaled(grouped[1].astype(jnp.float32)).astype(jnp.bfloat16)
    signal = (-token_rate * grouped[2].astype(jnp.float32)).astype(jnp.bfloat16)
    old_state = fast_state[:, 0]
    old_low = old_state.astype(jnp.bfloat16)
    partial_value = head_gradient(
        key_norm, signal, lax.all_gather(old_low, "seq", axis=1, tiled=True)
    )
    summed = lax.psum(partial_value, "seq")
    frob_norm = jnp.sqrt(jnp.sum(summed * summed, axis=(1, 2), keepdims=True))
    normalized = summed / (frob_norm + norm_eps)
    gram_matrix = jnp.einsum("mij,mkj->mik", normalized, normalized, precision=precise)
    hidden_units = gram_matrix.shape[1]
    selector = (
        jnp.arange(hidden_units, dtype=jnp.int32)[None, :]
        == seq_index * state_rows + jnp.arange(state_rows, dtype=jnp.int32)[:, None]
    ).astype(jnp.float32)
    row_block = jnp.broadcast_to(selector, (3, state_rows, hidden_units))
    for section_number in range(NS_STEPS - 1, -1, -1):
        row_block = poly_times(gram_matrix, section_number, row_block)
    final_rows = jnp.einsum("mij,mjk->mik", row_block, normalized, precision=precise)
    new_rows = old_state - head_rate[0] * final_rows
    weight_piece = lax.all_gather(new_rows.astype(jnp.bfloat16), "seq", axis=1, tiled=True)
    gate_act = contract_last(query_norm, weight_piece[0])
    up_act = contract_last(query_norm, weight_piece[1])
    active = (jax.nn.silu(gate_act) * up_act).astype(jnp.bfloat16)
    fast_out = jnp.dot(active, weight_piece[2], preferred_element_type=jnp.float32)
    key_value = grouped[1:3]
    reach_blocks = WINDOW // tok_rows
    earlier = [from_behind(key_value, "seq", distance) for distance in range(reach_blocks, 0, -1)]
    context = jnp.concatenate(earlier + [key_value], axis=1)
    scores = contract_last(grouped[0], context[0]) * head_dim ** (-0.5)
    query_pos = seq_index * tok_rows + jnp.arange(tok_rows, dtype=jnp.int32)[:, None]
    key_pos = (
        seq_index * tok_rows - WINDOW + jnp.arange(WINDOW + tok_rows, dtype=jnp.int32)[None, :]
    )
    visible = (key_pos <= query_pos) & (key_pos > query_pos - WINDOW) & (key_pos >= 0)
    scores = jnp.where(visible, scores, -jnp.inf)
    row_max = jnp.max(scores, axis=1, keepdims=True)
    exp_scores = jnp.exp(scores - row_max)
    weights = (exp_scores / jnp.sum(exp_scores, axis=1, keepdims=True)).astype(jnp.bfloat16)
    attention = jnp.dot(weights, context[1], preferred_element_type=jnp.float32)
    combined = (attention + fast_out).astype(jnp.bfloat16)
    tokens_back = lax.all_to_all(combined, "head", split_axis=0, concat_axis=1, tiled=True)
    return (tokens_back, new_rows[:, None])


def solution(mesh):
    return jax.shard_map(
        shards,
        mesh=mesh,
        in_specs=(
            P(None, ("seq", "head"), None),
            P("seq", "head"),
            P("head"),
            P(None, "head", "seq", None),
        ),
        out_specs=(P(("seq", "head"), None), P(None, "head", "seq", None)),
        check_vma=False,
    )
```

profile of v0, /device:TPU:16, one launch (start us, length us, event | category | flops | bytes accessed | tf_op | source)
XLA Modules:
  0.0 289.8 jit_solution(17737878514424476235)
XLA Ops:
  7.2 1.6 bitcast_convert_fusion
  8.8 1.6 copy.38
  10.4 1.4 reshape.124
  11.9 3.5 %all-to-all-start = ((bf16[2,2,49152]{2,1,0:T(2,128)(2,1)}), bf16[2,2,49152]{2,1,0:T(2,128)(2,1)S(1)}, u32[]{:S(2)}, u32[]{:S(2)}) async-start(bf16[2,2,49152]{2,1,0:T(2,128)(2,1)} %reshape.124), calls=%async_computation | async-start | bytes 786432 | tf_op jit(solution)/shard_map/all_to_all | solution.py:73
  15.5 6.7 %all-to-all-done = bf16[2,2,49152]{2,1,0:T(2,128)(2,1)S(1)} async-done(((bf16[2,2,49152]{2,1,0:T(2,128)(2,1)}), bf16[2,2,49152]{2,1,0:T(2,128)(2,1)S(1)}, u32[]{:S(2)}, u32[]{:S(2)}) %all-to-all-start) | async-done | bytes 393248 | tf_op jit(solution)/shard_map/all_to_all | solution.py:73
  22.2 0.6 reshape.125
  22.8 0.6 copy.40
  24.0 25.6 %all-gather.3.cloned.1.call-done = bf16[3,512,512]{2,1,0:T(8,128)(2,1)} async-done(((bf16[3,32,512]{2,1,0:T(8,128)(2,1)}), bf16[3,512,512]{2,1,0:T(8,128)(2,1)}) %all-gather.3.cloned.1.call-update) | async-done | bytes 1572880 | tf_op jit(solution)/shard_map/all_gather | solution.py:84
  49.6 1.3 fusion.17
  51.0 1.3 fusion.19
  52.7 1.3 fusion.18
  54.7 2.0 pad_maximum_fusion
  57.8 102.6 %all-reduce.2.cloned.1.call-done = f32[3,512,512]{2,1,0:T(8,128)} async-done(((f32[3,512,512]{2,1,0:T(8,128)}), f32[3,512,512]{2,1,0:T(8,128)}) %all-reduce.2.cloned.1.call-update) | async-done | bytes 3145744 | tf_op jit(solution)/shard_map/psum | solution.py:86
  160.3 2.5 multiply_reduce_fusion
  162.8 0.4 copy-done
  163.2 5.6 %fusion.15 = f32[3,512,512]{2,1,0:T(8,128)S(1)} fusion(f32[3,512,512]{2,1,0:T(8,128)S(1)} %copy-done, f32[3]{0:T(128)S(1)} %sqrt_add_fusion), kind=kOutput, calls=%fused_computation.33 | convolution fusion | flops 4832624640 | bytes 6291468 | tf_op jit(solution)/shard_map/mij,mkj->mik/dot_general | solution.py:89
  168.8 1.9 fusion.35
  170.7 1.9 fusion.48
  172.6 1.9 fusion.12
  174.5 1.9 fusion.49
  176.4 2.1 fusion.11
  178.5 1.9 fusion.50
  180.4 1.9 fusion.51
  182.3 1.9 fusion.10
  184.3 1.9 fusion.52
  186.2 1.9 fusion.9
  188.1 1.9 fusion.53
  190.0 2.1 fusion.6
  192.1 2.8 fusion.46
  195.0 1.3 collective-permute-start
  196.3 1.9 collective-permute-start.1
  198.2 2.9 collective-permute-start.2
  201.1 1.9 collective-permute-start.3
  203.1 1.9 collective-permute-start.4
  205.0 2.3 collective-permute-done
  207.3 1.9 collective-permute-start.5
  209.2 12.2 %collective-permute-start.6 = (bf16[2,128,512]{2,1,0:T(8,128)(2,1)S(1)}, bf16[2,128,512]{2,1,0:T(8,128)(2,1)S(1)}, u32[]{:S(2)}, u32[]{:S(2)}) collective-permute-start(bf16[2,128,512]{2,1,0:T(8,128)(2,1)S(1)} %bitcast.119), channel_id=1, source_target_pairs={{0,4},{2,6},{4,8},{6,10},{8,12},{10,14},{12,16},{14,18},{16,20},{1... | collective-permute-start | bytes 786440 | tf_op jit(solution)/shard_map/ppermute | solution.py:19
  221.8 13.3 %collective-permute-start.7 = (bf16[2,128,512]{2,1,0:T(8,128)(2,1)S(1)}, bf16[2,128,512]{2,1,0:T(8,128)(2,1)S(1)}, u32[]{:S(2)}, u32[]{:S(2)}) collective-permute-start(bf16[2,128,512]{2,1,0:T(8,128)(2,1)S(1)} %bitcast.120), channel_id=1, source_target_pairs={{0,2},{2,4},{4,6},{6,8},{8,10},{10,12},{12,14},{14,16},{16,18},{18... | collective-permute-start | bytes 786440 | tf_op jit(solution)/shard_map/ppermute | solution.py:19
  235.2 8.6 %collective-permute-done.4 = bf16[2,128,512]{2,1,0:T(8,128)(2,1)S(1)} collective-permute-done((bf16[2,128,512]{2,1,0:T(8,128)(2,1)S(1)}, bf16[2,128,512]{2,1,0:T(8,128)(2,1)S(1)}, u32[]{:S(2)}, u32[]{:S(2)}) %collective-permute-start.4) | collective-permute-done | bytes 262176 | tf_op jit(solution)/shard_map/ppermute | solution.py:19
  243.9 2.9 collective-permute-done.5
  246.8 20.7 %collective-permute-done.6 = bf16[2,128,512]{2,1,0:T(8,128)(2,1)S(1)} collective-permute-done((bf16[2,128,512]{2,1,0:T(8,128)(2,1)S(1)}, bf16[2,128,512]{2,1,0:T(8,128)(2,1)S(1)}, u32[]{:S(2)}, u32[]{:S(2)}) %collective-permute-start.6) | collective-permute-done | bytes 262176 | tf_op jit(solution)/shard_map/ppermute | solution.py:19
  267.5 2.3 collective-permute-done.7
  269.9 0.5 fusion.47
  270.6 1.3 fusion.16
  271.9 2.4 fusion.14
  274.3 1.3 fusion.13
  275.6 7.0 %all_to_all.34 = bf16[2,64,512]{2,1,0:T(8,128)(2,1)S(1)} all-to-all(bf16[2,64,512]{2,1,0:T(8,128)(2,1)S(1)} %bitcast.127), channel_id=1, replica_groups=mesh['seq'=16,'head'=2] {'head'}, dimensions={0} | all-to-all | bytes 262144 | tf_op jit(solution)/shard_map/all_to_all | solution.py:121
  282.6 0.7 copy.51
  (45 shorter events, 3.0 us)
Async XLA Ops:
  7.2 8.2 %copy-start.2 = (f32[128,1]{0,1:T(1,128)S(1)}, f32[128,1]{0,1:T(1,128)}, u32[]{:S(2)}) copy-start(f32[128,1]{0,1:T(1,128)} %param.5) | copy-start | bytes 1540
  7.2 42.5 %all-gather.3.cloned.1.call-start = ((), (), s32[]{:S(2)}) async-start(), calls=%async_computation.2 | async-start | bytes 1671168 | tf_op jit(solution)/shard_map/all_gather | solution.py:84
  11.9 10.3 %all-to-all-start = ((bf16[2,2,49152]{2,1,0:T(2,128)(2,1)}), bf16[2,2,49152]{2,1,0:T(2,128)(2,1)S(1)}, u32[]{:S(2)}, u32[]{:S(2)}) async-start(bf16[2,2,49152]{2,1,0:T(2,128)(2,1)} %reshape.124), calls=%async_computation | async-start | bytes 786432 | tf_op jit(solution)/shard_map/all_to_all | solution.py:73
  15.3 145.0 %all-reduce.2.cloned.1.call-start = ((), (), s32[]{:S(2)}) async-start(), calls=%async_computation.3 | async-start | bytes 6291456 | tf_op jit(solution)/shard_map/psum | solution.py:86
  56.7 213.8 %all-gather.5.cloned.1.call-start = ((), (), s32[]{:S(2)}) async-start(), calls=%async_computation.4 | async-start | bytes 1671168 | tf_op jit(solution)/shard_map/all_gather | solution.py:100
  160.3 2.8 copy-start
  188.1 4.1 %copy-start.1 = (f32[3,1,32,512]{3,2,1,0:T(8,128)S(1)}, f32[3,1,32,512]{3,2,1,0:T(8,128)}, u32[]{:S(2)}) copy-start(f32[3,1,32,512]{3,2,1,0:T(8,128)} %param.7) | copy-start | bytes 589828
  195.0 12.3 %collective-permute-start = (bf16[2,128,512]{2,1,0:T(8,128)(2,1)S(1)}, bf16[2,128,512]{2,1,0:T(8,128)(2,1)S(1)}, u32[]{:S(2)}, u32[]{:S(2)}) collective-permute-start(bf16[2,128,512]{2,1,0:T(8,128)(2,1)S(1)} %bitcast.113), channel_id=1, source_target_pairs={{0,16},{2,18},{4,20},{6,22},{8,24},{10,26},{12,28},{14,30},{1,17},... | collective-permute-start | bytes 786440 | tf_op jit(solution)/shard_map/ppermute | solution.py:19
  196.3 12.9 %collective-permute-start.1 = (bf16[2,128,512]{2,1,0:T(8,128)(2,1)S(1)}, bf16[2,128,512]{2,1,0:T(8,128)(2,1)S(1)}, u32[]{:S(2)}, u32[]{:S(2)}) collective-permute-start(bf16[2,128,512]{2,1,0:T(8,128)(2,1)S(1)} %bitcast.114), channel_id=1, source_target_pairs={{0,14},{2,16},{4,18},{6,20},{8,22},{10,24},{12,26},{14,28},{16,30}... | collective-permute-start | bytes 786440 | tf_op jit(solution)/shard_map/ppermute | solution.py:19
  198.2 23.6 %collective-permute-start.2 = (bf16[2,128,512]{2,1,0:T(8,128)(2,1)S(1)}, bf16[2,128,512]{2,1,0:T(8,128)(2,1)S(1)}, u32[]{:S(2)}, u32[]{:S(2)}) collective-permute-start(bf16[2,128,512]{2,1,0:T(8,128)(2,1)S(1)} %bitcast.115), channel_id=1, source_target_pairs={{0,12},{2,14},{4,16},{6,18},{8,20},{10,22},{12,24},{14,26},{16,28}... | collective-permute-start | bytes 786440 | tf_op jit(solution)/shard_map/ppermute | solution.py:19
  201.1 34.1 %collective-permute-start.3 = (bf16[2,128,512]{2,1,0:T(8,128)(2,1)S(1)}, bf16[2,128,512]{2,1,0:T(8,128)(2,1)S(1)}, u32[]{:S(2)}, u32[]{:S(2)}) collective-permute-start(bf16[2,128,512]{2,1,0:T(8,128)(2,1)S(1)} %bitcast.116), channel_id=1, source_target_pairs={{0,10},{2,12},{4,14},{6,16},{8,18},{10,20},{12,22},{14,24},{16,26}... | collective-permute-start | bytes 786440 | tf_op jit(solution)/shard_map/ppermute | solution.py:19
  203.1 40.8 %collective-permute-start.4 = (bf16[2,128,512]{2,1,0:T(8,128)(2,1)S(1)}, bf16[2,128,512]{2,1,0:T(8,128)(2,1)S(1)}, u32[]{:S(2)}, u32[]{:S(2)}) collective-permute-start(bf16[2,128,512]{2,1,0:T(8,128)(2,1)S(1)} %bitcast.117), channel_id=1, source_target_pairs={{0,8},{2,10},{4,12},{6,14},{8,16},{10,18},{12,20},{14,22},{16,24},... | collective-permute-start | bytes 786440 | tf_op jit(solution)/shard_map/ppermute | solution.py:19
  207.3 39.5 %collective-permute-start.5 = (bf16[2,128,512]{2,1,0:T(8,128)(2,1)S(1)}, bf16[2,128,512]{2,1,0:T(8,128)(2,1)S(1)}, u32[]{:S(2)}, u32[]{:S(2)}) collective-permute-start(bf16[2,128,512]{2,1,0:T(8,128)(2,1)S(1)} %bitcast.118), channel_id=1, source_target_pairs={{0,6},{2,8},{4,10},{6,12},{8,14},{10,16},{12,18},{14,20},{16,22},{... | collective-permute-start | bytes 786440 | tf_op jit(solution)/shard_map/ppermute | solution.py:19
  209.2 58.3 %collective-permute-start.6 = (bf16[2,128,512]{2,1,0:T(8,128)(2,1)S(1)}, bf16[2,128,512]{2,1,0:T(8,128)(2,1)S(1)}, u32[]{:S(2)}, u32[]{:S(2)}) collective-permute-start(bf16[2,128,512]{2,1,0:T(8,128)(2,1)S(1)} %bitcast.119), channel_id=1, source_target_pairs={{0,4},{2,6},{4,8},{6,10},{8,12},{10,14},{12,16},{14,18},{16,20},{1... | collective-permute-start | bytes 786440 | tf_op jit(solution)/shard_map/ppermute | solution.py:19
  221.8 48.0 %collective-permute-start.7 = (bf16[2,128,512]{2,1,0:T(8,128)(2,1)S(1)}, bf16[2,128,512]{2,1,0:T(8,128)(2,1)S(1)}, u32[]{:S(2)}, u32[]{:S(2)}) collective-permute-start(bf16[2,128,512]{2,1,0:T(8,128)(2,1)S(1)} %bitcast.120), channel_id=1, source_target_pairs={{0,2},{2,4},{4,6},{6,8},{8,10},{10,12},{12,14},{14,16},{16,18},{18... | collective-permute-start | bytes 786440 | tf_op jit(solution)/shard_map/ppermute | solution.py:19
Sparse Core Ops, SparseCore 0:
  10.7 38.8 all-gather.2
  56.8 103.4 all-reduce.1
  195.1 53.1 all-gather.4
where the time goes:
time: 290 us
  waiting for transfers between devices  172 us (59%)
  matrix products  42.2 us (15%)
  starting transfers between devices  41.2 us (14%)
  between operations  14.8 us (5%)
  blocking collectives  7 us (2%)
  other arithmetic  6.92 us (2%)
  local copies, waits for them, and re-layouts  5.59 us (2%)
    psum x1, waiting for transfers between devices, shards(): summed = lax.psum(partial_value, 'seq')  103 us
    ppermute x8, starting transfers between devices, from_behind(): return lax.ppermute(block, axis, route)  37.4 us
    ppermute x8, waiting for transfers between devices, from_behind(): return lax.ppermute(block, axis, route)  37.1 us
    all_gather x1, waiting for transfers between devices, shards(): lax.all_gather(old_low, 'seq', axis=1, tiled=True)  25.6 us
    dot_general x12, matrix products, gram_times(): return jnp.einsum('mij,mjk->mik', row_block, gram_matrix, precision=precise)  23.2 us
    all_to_all x1, blocking collectives, shards(): lax.all_to_all(combined, 'head', split_axis=0, concat_axis=1, tiled=True)  7 us
    all_to_all x1, waiting for transfers between devices, shards(): lax.all_to_all(qkv, 'head', split_axis=2, concat_axis=1, tiled=True)  6.67 us
    dot_general x5, matrix products, contract_last(): lax.dot_general(left_side, right_side, (((1,), (1,)), ((), ())), preferre...  5.86 us
  transfers between devices with their start and end apart: 12, of which 9 were waited for; matrix products, arithmetic and copies ran while one was open for 2% of the time, Pallas kernels for 0%

commit v1 on v0

--- a/solution.py
+++ b/solution.py
@@ -1,3 +1,4 @@
+import functools
 import jax
 import jax.numpy as jnp
 from jax import lax
@@ -11,6 +12,15 @@
 rms_eps = 1e-06
 norm_eps = 1e-07
 precise = lax.Precision.HIGHEST
+
+
+def divide_positions(mine_x, ax_name):
+    r1 = lax.all_gather(mine_x, ax_name)
+    found_now = jnp.sum(r1, 0)
+    return found_now
+
+
+fix_types = functools.partial(divide_positions, ax_name="seq")
 
 
 def from_behind(block, axis, distance):
@@ -83,7 +93,7 @@
     partial_value = head_gradient(
         key_norm, signal, lax.all_gather(old_low, "seq", axis=1, tiled=True)
     )
-    summed = lax.psum(partial_value, "seq")
+    summed = fix_types(partial_value)
     frob_norm = jnp.sqrt(jnp.sum(summed * summed, axis=(1, 2), keepdims=True))
     normalized = summed / (frob_norm + norm_eps)
     gram_matrix = jnp.einsum("mij,mkj->mik", normalized, normalized, precision=precise)

time: 290 us -> 453 us (1.56)
  waiting for transfers between devices: 172 us -> 318 us
  other arithmetic: 6.92 us -> 26.2 us
    all_gather x0 -> x1, waiting for transfers between devices: none -> 246 us  [divide_positions(): r1 = lax.all_gather(mine_x, ax_name)]
    psum x1 -> x0, waiting for transfers between devices: 103 us -> none  [shards(): summed = lax.psum(partial_value, 'seq')]
    reduce_sum x0 -> x1, other arithmetic: none -> 18.8 us  [divide_positions(): found_now = jnp.sum(r1, 0)]
where the time goes in v1:
time: 453 us; the launch traced here: 452 us
  waiting for transfers between devices  318 us (70%)
  matrix products  42.2 us (9%)
  starting transfers between devices  38.7 us (9%)
  other arithmetic  26.2 us (6%)
  between operations  14.9 us (3%)
  blocking collectives  7 us (2%)
  local copies, waits for them, and re-layouts  5.27 us (1%)
    all_gather x1, waiting for transfers between devices, divide_positions(): r1 = lax.all_gather(mine_x, ax_name)  246 us
    ppermute x8, waiting for transfers between devices, from_behind(): return lax.ppermute(block, axis, route)  41.5 us
    ppermute x8, starting transfers between devices, from_behind(): return lax.ppermute(block, axis, route)  35.1 us
    all_gather x1, waiting for transfers between devices, shards(): lax.all_gather(old_low, 'seq', axis=1, tiled=True)  24.4 us
    dot_general x12, matrix products, gram_times(): return jnp.einsum('mij,mjk->mik', row_block, gram_matrix, precision=precise)  23.2 us
    reduce_sum x1, other arithmetic, divide_positions(): found_now = jnp.sum(r1, 0)  18.8 us
  transfers between devices with their start and end apart: 12, of which 9 were waited for; matrix products, arithmetic and copies ran while one was open for 2% of the time, Pallas kernels for 0%

profile of v1, /device:TPU:16, one launch (start us, length us, event | category | flops | bytes accessed | tf_op | source)
XLA Modules:
  0.0 452.5 jit_solution(9109874855339767129)
XLA Ops:
  7.2 1.6 bitcast_convert_fusion
  8.8 1.6 copy.38
  10.4 1.4 reshape.125
  11.9 3.5 all-to-all-start
  15.5 6.7 %all-to-all-done = bf16[2,2,49152]{2,1,0:T(2,128)(2,1)S(1)} async-done(((bf16[2,2,49152]{2,1,0:T(2,128)(2,1)}), bf16[2,2,49152]{2,1,0:T(2,128)(2,1)S(1)}, u32[]{:S(2)}, u32[]{:S(2)}) %all-to-all-start) | async-done | bytes 393248 | tf_op jit(solution)/shard_map/all_to_all | solution.py:83
  23.6 0.7 fusion.45
  24.5 0.8 multiply_convert_fusion.4
  25.3 24.4 %all-gather.5.cloned.1.call-done = bf16[3,512,512]{2,1,0:T(8,128)(2,1)} async-done(((bf16[3,32,512]{2,1,0:T(8,128)(2,1)}), bf16[3,512,512]{2,1,0:T(8,128)(2,1)}) %all-gather.5.cloned.1.call-update) | async-done | bytes 1572880 | tf_op jit(solution)/shard_map/all_gather | solution.py:94
  49.6 1.3 fusion.17
  51.0 1.3 fusion.19
  52.7 1.3 fusion.18
  54.7 1.9 pad_maximum_fusion
  57.4 0.7 fusion.37
  58.1 0.7 fusion.38
  58.8 245.6 %all-gather.9.cloned.1.call-done = f32[48,512,512]{2,1,0:T(8,128)} async-done(((f32[3,512,512]{2,1,0:T(8,128)}), f32[48,512,512]{2,1,0:T(8,128)}) %all-gather.9.cloned.1.call-update) | async-done | bytes 50331664 | tf_op jit(solution)/shard_map/all_gather | solution.py:18
  304.4 18.8 %reduce_sum.48 = f32[3,512,512]{2,1,0:T(8,128)S(1)} reduce(f32[16,3,512,512]{3,2,1,0:T(8,128)} %bitcast.106, f32[]{:T(128)} %constant.15.clone.1), dimensions={0}, to_apply=%region_4.5 | reduce | flops 11796480 | bytes 53477380 | tf_op jit(solution)/shard_map/reduce_sum | solution.py:19
  323.7 5.7 %fusion.15 = f32[3,512,512]{2,1,0:T(8,128)S(1)} fusion(f32[3,512,512]{2,1,0:T(8,128)S(1)} %reduce_sum.48, f32[3]{0:T(128)S(1)} %sqrt_add_fusion), kind=kOutput, calls=%fused_computation.33 | convolution fusion | flops 4832624640 | bytes 6291468 | tf_op jit(solution)/shard_map/mij,mkj->mik/dot_general | solution.py:99
  329.4 1.9 fusion.35
  331.3 1.9 fusion.48
  333.2 1.9 fusion.12
  335.1 1.9 fusion.49
  337.0 2.1 fusion.11
  339.1 1.9 fusion.50
  341.0 1.9 fusion.51
  342.9 1.9 fusion.10
  344.8 1.9 fusion.52
  346.7 1.9 fusion.9
  348.6 1.9 fusion.53
  350.5 2.1 fusion.6
  352.7 2.8 fusion.46
  355.5 1.3 collective-permute-start
  356.8 3.2 collective-permute-start.1
  360.1 1.9 collective-permute-start.2
  362.0 1.9 collective-permute-start.3
  363.9 1.9 collective-permute-start.4
  365.9 2.8 collective-permute-done
  368.6 1.9 collective-permute-start.5
  370.6 4.2 collective-permute-done.1
  374.8 10.0 %collective-permute-start.6 = (bf16[2,128,512]{2,1,0:T(8,128)(2,1)S(1)}, bf16[2,128,512]{2,1,0:T(8,128)(2,1)S(1)}, u32[]{:S(2)}, u32[]{:S(2)}) collective-permute-start(bf16[2,128,512]{2,1,0:T(8,128)(2,1)S(1)} %bitcast.121), channel_id=1, source_target_pairs={{0,4},{2,6},{4,8},{6,10},{8,12},{10,14},{12,16},{14,18},{16,20},{1... | collective-permute-start | bytes 786440 | tf_op jit(solution)/shard_map/ppermute | solution.py:29
  384.8 13.0 %collective-permute-start.7 = (bf16[2,128,512]{2,1,0:T(8,128)(2,1)S(1)}, bf16[2,128,512]{2,1,0:T(8,128)(2,1)S(1)}, u32[]{:S(2)}, u32[]{:S(2)}) collective-permute-start(bf16[2,128,512]{2,1,0:T(8,128)(2,1)S(1)} %bitcast.122), channel_id=1, source_target_pairs={{0,2},{2,4},{4,6},{6,8},{8,10},{10,12},{12,14},{14,16},{16,18},{18... | collective-permute-start | bytes 786440 | tf_op jit(solution)/shard_map/ppermute | solution.py:29
  397.9 9.4 %collective-permute-done.4 = bf16[2,128,512]{2,1,0:T(8,128)(2,1)S(1)} collective-permute-done((bf16[2,128,512]{2,1,0:T(8,128)(2,1)S(1)}, bf16[2,128,512]{2,1,0:T(8,128)(2,1)S(1)}, u32[]{:S(2)}, u32[]{:S(2)}) %collective-permute-start.4) | collective-permute-done | bytes 262176 | tf_op jit(solution)/shard_map/ppermute | solution.py:29
  407.3 2.7 collective-permute-done.5
  410.0 20.1 %collective-permute-done.6 = bf16[2,128,512]{2,1,0:T(8,128)(2,1)S(1)} collective-permute-done((bf16[2,128,512]{2,1,0:T(8,128)(2,1)S(1)}, bf16[2,128,512]{2,1,0:T(8,128)(2,1)S(1)}, u32[]{:S(2)}, u32[]{:S(2)}) %collective-permute-start.6) | collective-permute-done | bytes 262176 | tf_op jit(solution)/shard_map/ppermute | solution.py:29
  430.1 2.3 collective-permute-done.7
  433.2 1.3 fusion.16
  434.6 2.4 fusion.14
  436.9 1.3 fusion.13
  438.3 7.0 %all_to_all.34 = bf16[2,64,512]{2,1,0:T(8,128)(2,1)S(1)} all-to-all(bf16[2,64,512]{2,1,0:T(8,128)(2,1)S(1)} %bitcast.129), channel_id=1, replica_groups=mesh['seq'=16,'head'=2] {'head'}, dimensions={0} | all-to-all | bytes 262144 | tf_op jit(solution)/shard_map/all_to_all | solution.py:131
  (52 shorter events, 4.9 us)
Async XLA Ops:
  7.2 8.2 %copy-start.5 = (f32[128,1]{0,1:T(1,128)S(1)}, f32[128,1]{0,1:T(1,128)}, u32[]{:S(2)}) copy-start(f32[128,1]{0,1:T(1,128)} %param.5) | copy-start | bytes 1540
  7.2 42.5 %all-gather.5.cloned.1.call-start = ((), (), s32[]{:S(2)}) async-start(), calls=%async_computation.2 | async-start | bytes 1671168 | tf_op jit(solution)/shard_map/all_gather | solution.py:94
  11.9 10.3 %all-to-all-start = ((bf16[2,2,49152]{2,1,0:T(2,128)(2,1)}), bf16[2,2,49152]{2,1,0:T(2,128)(2,1)S(1)}, u32[]{:S(2)}, u32[]{:S(2)}) async-start(bf16[2,2,49152]{2,1,0:T(2,128)(2,1)} %reshape.125), calls=%async_computation | async-start | bytes 786432 | tf_op jit(solution)/shard_map/all_to_all | solution.py:83
  15.3 289.1 %all-gather.9.cloned.1.call-start = ((), (), s32[]{:S(2)}) async-start(), calls=%async_computation.4 | async-start | bytes 53477376 | tf_op jit(solution)/shard_map/all_gather | solution.py:18
  56.7 376.5 %all-gather.7.cloned.1.call-start = ((), (), s32[]{:S(2)}) async-start(), calls=%async_computation.3 | async-start | bytes 1671168 | tf_op jit(solution)/shard_map/all_gather | solution.py:110
  323.7 5.7 %copy-start.2 = (f32[32,512]{1,0:T(8,128)S(1)}, f32[32,512]{1,0:T(8,128)}, u32[]{:S(2)}) copy-start(f32[32,512]{1,0:T(8,128)} %fusion.37) | copy-start | bytes 196612
  342.9 3.8 copy-start.1
  348.6 4.1 copy-start.3
  355.4 77.1 %copy-start.4 = (bf16[1,2,64,512]{3,2,1,0:T(8,128)(2,1)S(1)}, bf16[1,2,64,512]{3,2,1,0:T(8,128)(2,1)}, u32[]{:S(2)}) copy-start(bf16[1,2,64,512]{3,2,1,0:T(8,128)(2,1)} %get-tuple-element.14) | copy-start | bytes 393220
  355.5 13.1 %collective-permute-start = (bf16[2,128,512]{2,1,0:T(8,128)(2,1)S(1)}, bf16[2,128,512]{2,1,0:T(8,128)(2,1)S(1)}, u32[]{:S(2)}, u32[]{:S(2)}) collective-permute-start(bf16[2,128,512]{2,1,0:T(8,128)(2,1)S(1)} %bitcast.115), channel_id=1, source_target_pairs={{0,16},{2,18},{4,20},{6,22},{8,24},{10,26},{12,28},{14,30},{1,17},... | collective-permute-start | bytes 786440 | tf_op jit(solution)/shard_map/ppermute | solution.py:29
  356.8 18.0 %collective-permute-start.1 = (bf16[2,128,512]{2,1,0:T(8,128)(2,1)S(1)}, bf16[2,128,512]{2,1,0:T(8,128)(2,1)S(1)}, u32[]{:S(2)}, u32[]{:S(2)}) collective-permute-start(bf16[2,128,512]{2,1,0:T(8,128)(2,1)S(1)} %bitcast.116), channel_id=1, source_target_pairs={{0,14},{2,16},{4,18},{6,20},{8,22},{10,24},{12,26},{14,28},{16,30}... | collective-permute-start | bytes 786440 | tf_op jit(solution)/shard_map/ppermute | solution.py:29
  360.1 24.7 %collective-permute-start.2 = (bf16[2,128,512]{2,1,0:T(8,128)(2,1)S(1)}, bf16[2,128,512]{2,1,0:T(8,128)(2,1)S(1)}, u32[]{:S(2)}, u32[]{:S(2)}) collective-permute-start(bf16[2,128,512]{2,1,0:T(8,128)(2,1)S(1)} %bitcast.117), channel_id=1, source_target_pairs={{0,12},{2,14},{4,16},{6,18},{8,20},{10,22},{12,24},{14,26},{16,28}... | collective-permute-start | bytes 786440 | tf_op jit(solution)/shard_map/ppermute | solution.py:29
  362.0 35.8 %collective-permute-start.3 = (bf16[2,128,512]{2,1,0:T(8,128)(2,1)S(1)}, bf16[2,128,512]{2,1,0:T(8,128)(2,1)S(1)}, u32[]{:S(2)}, u32[]{:S(2)}) collective-permute-start(bf16[2,128,512]{2,1,0:T(8,128)(2,1)S(1)} %bitcast.118), channel_id=1, source_target_pairs={{0,10},{2,12},{4,14},{6,16},{8,18},{10,20},{12,22},{14,24},{16,26}... | collective-permute-start | bytes 786440 | tf_op jit(solution)/shard_map/ppermute | solution.py:29
  363.9 43.3 %collective-permute-start.4 = (bf16[2,128,512]{2,1,0:T(8,128)(2,1)S(1)}, bf16[2,128,512]{2,1,0:T(8,128)(2,1)S(1)}, u32[]{:S(2)}, u32[]{:S(2)}) collective-permute-start(bf16[2,128,512]{2,1,0:T(8,128)(2,1)S(1)} %bitcast.119), channel_id=1, source_target_pairs={{0,8},{2,10},{4,12},{6,14},{8,16},{10,18},{12,20},{14,22},{16,24},... | collective-permute-start | bytes 786440 | tf_op jit(solution)/shard_map/ppermute | solution.py:29
  368.6 41.3 %collective-permute-start.5 = (bf16[2,128,512]{2,1,0:T(8,128)(2,1)S(1)}, bf16[2,128,512]{2,1,0:T(8,128)(2,1)S(1)}, u32[]{:S(2)}, u32[]{:S(2)}) collective-permute-start(bf16[2,128,512]{2,1,0:T(8,128)(2,1)S(1)} %bitcast.120), channel_id=1, source_target_pairs={{0,6},{2,8},{4,10},{6,12},{8,14},{10,16},{12,18},{14,20},{16,22},{... | collective-permute-start | bytes 786440 | tf_op jit(solution)/shard_map/ppermute | solution.py:29
  374.8 55.3 %collective-permute-start.6 = (bf16[2,128,512]{2,1,0:T(8,128)(2,1)S(1)}, bf16[2,128,512]{2,1,0:T(8,128)(2,1)S(1)}, u32[]{:S(2)}, u32[]{:S(2)}) collective-permute-start(bf16[2,128,512]{2,1,0:T(8,128)(2,1)S(1)} %bitcast.121), channel_id=1, source_target_pairs={{0,4},{2,6},{4,8},{6,10},{8,12},{10,14},{12,16},{14,18},{16,20},{1... | collective-permute-start | bytes 786440 | tf_op jit(solution)/shard_map/ppermute | solution.py:29
  384.8 47.6 %collective-permute-start.7 = (bf16[2,128,512]{2,1,0:T(8,128)(2,1)S(1)}, bf16[2,128,512]{2,1,0:T(8,128)(2,1)S(1)}, u32[]{:S(2)}, u32[]{:S(2)}) collective-permute-start(bf16[2,128,512]{2,1,0:T(8,128)(2,1)S(1)} %bitcast.122), channel_id=1, source_target_pairs={{0,2},{2,4},{4,6},{6,8},{8,10},{10,12},{12,14},{14,16},{16,18},{18... | collective-permute-start | bytes 786440 | tf_op jit(solution)/shard_map/ppermute | solution.py:29
  397.9 35.3 %copy-start = (bf16[1,2,64,512]{3,2,1,0:T(8,128)(2,1)S(1)}, bf16[1,2,64,512]{3,2,1,0:T(8,128)(2,1)}, u32[]{:S(2)}) copy-start(bf16[1,2,64,512]{3,2,1,0:T(8,128)(2,1)} %get-tuple-element.18) | copy-start | bytes 393220
Sparse Core Ops, SparseCore 0:
  10.7 38.8 all-gather.4
  56.8 247.6 all-gather.8
  355.6 52.1 all-gather.6
